TPU v7x, 32 devices: a whole 2x2x4 slice. The times are simulated.
32 devices in a mesh: clip: 2 (over core), tm: 16 (over z, y, x).
Axes of the slice: x: 2, y: 2, z: 4, core: 2. Of those that a mesh axis runs over, the one named last changes fastest.
Arguments:
- clip_frames: bfloat16 [2, 32, 64, 64, 128], P('clip', 'tm'), may hold values from -6 to 6
- spatial_weight: bfloat16 [3, 3, 128, 256], replicated, may hold values from -0.1875 to 0.1875
- norm_gain: float32 [256], replicated, may hold values from 0.5 to 1.5
- norm_bias: float32 [256], replicated, may hold values from -3 to 3
- temporal_weight: bfloat16 [3, 256, 256], replicated, may hold values from -0.21875 to 0.21875
- cotangent: bfloat16 [2, 32, 32, 32, 256], P('clip', 'tm'), may hold values from -0.0234375 to 0.0234375
Outputs:
- mixed: bfloat16 [2, 32, 32, 32, 256], P('clip', 'tm')
- spatial_grad: float32 [3, 3, 128, 256], replicated
- gain_grad: float32 [256], replicated
- bias_grad: float32 [256], replicated
- temporal_grad: float32 [3, 256, 256], replicated
All inputs are finite; a program needn't handle non-finite values.
Results may differ from a plain program's by a relative error of at most 0.0085.
Values may be sent and summed in bfloat16 or wider, within the bound.
A program may use at most 64 MiB of HBM per device.

v0:
```python
import jax
import jax.numpy as jnp
from jax import lax
from jax.sharding import PartitionSpec as P

GROUPS = 32
DILATION_FRAMES = 4
epsilon = 1e-05


def delay_rows(values):
    return jnp.pad(values, ((0, 0), (1, 0), (0, 0), (0, 0)))[:, :-1]


def delay_cols(values):
    return jnp.pad(values, ((0, 0), (0, 0), (1, 0), (0, 0)))[:, :, :-1]


def advance_rows(values):
    return jnp.pad(values, ((0, 0), (0, 1), (0, 0), (0, 0)))[:, 1:]


def advance_cols(values):
    return jnp.pad(values, ((0, 0), (0, 0), (0, 1), (0, 0)))[:, :, 1:]


def split_phases(frames_in):
    frames, height, width, chans = frames_in.shape
    viewed = frames_in.reshape(frames, height // 2, 2, width // 2, 2, chans)
    phases = {}
    for row_phase in range(2):
        for col_phase in range(2):
            phases[row_phase, col_phase] = viewed[:, :, row_phase, :, col_phase, :].reshape(
                -1, chans
            )
    return phases


def tap_layout(offset):
    return (0 if offset == 1 else 1, offset == 0)


def membership(chans):
    channel_group = lax.broadcasted_iota(jnp.int32, (chans, GROUPS), 0) // (chans // GROUPS)
    group_index = lax.broadcasted_iota(jnp.int32, (chans, GROUPS), 1)
    return (channel_group == group_index).astype(jnp.float32)


def activate(conv_out, gain, bias):
    chans = conv_out.shape[-1]
    member = membership(chans)
    count = conv_out.shape[1] * conv_out.shape[2] * (chans // GROUPS)
    high = lax.Precision.HIGHEST
    chan_sum = jnp.sum(conv_out, axis=(1, 2))
    group_mean = jnp.dot(chan_sum, member, precision=high) / count
    center = jnp.dot(group_mean, member.T, precision=high)
    deviation = conv_out - center[:, None, None, :]
    chan_square = jnp.sum(deviation * deviation, axis=(1, 2))
    group_var = jnp.dot(chan_square, member, precision=high) / count
    scaling = jnp.dot(lax.rsqrt(group_var + epsilon), member.T, precision=high)
    normed = deviation * scaling[:, None, None, :]
    return jax.nn.silu(normed * gain + bias)


def padded_lag(values, frame_offset):
    if frame_offset == 0:
        return values
    frames = values.shape[0]
    if frame_offset > 0:
        filler = jnp.zeros((frame_offset,) + values.shape[1:], values.dtype)
        return jnp.concatenate([filler, values[: frames - frame_offset]], axis=0)
    filler = jnp.zeros((-frame_offset,) + values.shape[1:], values.dtype)
    return jnp.concatenate([values[-frame_offset:], filler], axis=0)


def temporal_pass(acts, grads, weight, lag_rule):
    chans = acts.shape[-1]
    total = acts.astype(jnp.float32)
    backward_total_sum = grads.astype(jnp.float32)
    tap_grads = []
    flattened_gradients = grads.reshape(-1, chans)
    for kernel_tap_index in range(3):
        frame_offset = kernel_tap_index * DILATION_FRAMES
        earlier = lag_rule(acts, frame_offset).reshape(-1, chans)
        later = lag_rule(grads, -frame_offset).reshape(-1, chans)
        total = total + jnp.dot(
            earlier, weight[kernel_tap_index], preferred_element_type=jnp.float32
        ).reshape(acts.shape)
        backward_total_sum = backward_total_sum + jnp.dot(
            later, weight[kernel_tap_index].T, preferred_element_type=jnp.float32
        ).reshape(acts.shape)
        tap_grads.append(
            lax.dot_general(
                earlier,
                flattened_gradients,
                (((0,), (0,)), ((), ())),
                preferred_element_type=jnp.float32,
            )
        )
    return (
        total.astype(jnp.bfloat16),
        backward_total_sum.astype(jnp.bfloat16),
        jnp.stack(tap_grads),
    )


def per_device(clip_frames, spatial_weight, norm_gain, norm_bias, temporal_weight, cotangent):
    frames_in = clip_frames[0]
    upstream = cotangent[0]
    frames, height, width, _ = frames_in.shape
    out_chans = spatial_weight.shape[-1]
    out_shape = (frames, height // 2, width // 2, out_chans)
    phases = split_phases(frames_in)
    partial_sums = {}
    for row_offset in range(3):
        row_phase, row_delay = tap_layout(row_offset)
        for col_offset in range(3):
            col_phase, col_delay = tap_layout(col_offset)
            product = jnp.dot(
                phases[row_phase, col_phase],
                spatial_weight[row_offset, col_offset],
                preferred_element_type=jnp.float32,
            )
            key_pair = (row_delay, col_delay)
            if key_pair in partial_sums:
                partial_sums[key_pair] = partial_sums[key_pair] + product
            else:
                partial_sums[key_pair] = product
    conv_out = partial_sums[False, False].reshape(out_shape)
    conv_out = conv_out + delay_rows(partial_sums[True, False].reshape(out_shape))
    conv_out = conv_out + delay_cols(partial_sums[False, True].reshape(out_shape))
    conv_out = conv_out + delay_rows(delay_cols(partial_sums[True, True].reshape(out_shape)))
    activated, pullback = jax.vjp(activate, conv_out, norm_gain, norm_bias)
    acts = activated.astype(jnp.bfloat16)
    act_rows = lax.all_to_all(acts, "tm", split_axis=1, concat_axis=0, tiled=True)
    grad_rows = lax.all_to_all(upstream, "tm", split_axis=1, concat_axis=0, tiled=True)
    mixed_rows, act_grad_rows, temporal_part = temporal_pass(
        act_rows, grad_rows, temporal_weight, padded_lag
    )
    mixed = lax.all_to_all(mixed_rows, "tm", split_axis=0, concat_axis=1, tiled=True)
    act_grad = lax.all_to_all(act_grad_rows, "tm", split_axis=0, concat_axis=1, tiled=True)
    conv_grad, gain_partial_sum, bias_part = pullback(act_grad.astype(jnp.float32))
    conv_grad = conv_grad.astype(jnp.bfloat16)
    grad_versions = {
        (False, False): conv_grad.reshape(-1, out_chans),
        (True, False): advance_rows(conv_grad).reshape(-1, out_chans),
        (False, True): advance_cols(conv_grad).reshape(-1, out_chans),
        (True, True): advance_rows(advance_cols(conv_grad)).reshape(-1, out_chans),
    }
    tap_rows = []
    for row_offset in range(3):
        row_phase, row_delay = tap_layout(row_offset)
        tap_row = []
        for col_offset in range(3):
            col_phase, col_delay = tap_layout(col_offset)
            tap_row.append(
                lax.dot_general(
                    phases[row_phase, col_phase],
                    grad_versions[row_delay, col_delay],
                    (((0,), (0,)), ((), ())),
                    preferred_element_type=jnp.float32,
                )
            )
        tap_rows.append(jnp.stack(tap_row))
    spatial_part = jnp.stack(tap_rows)
    spatial_gradient_total, gain_total, bias_total, temporal_total = lax.psum(
        (spatial_part, gain_partial_sum, bias_part, temporal_part), ("clip", "tm")
    )
    return (mixed[None], spatial_gradient_total, gain_total, bias_total, temporal_total)


def solution(mesh):
    return jax.shard_map(
        per_device,
        mesh=mesh,
        in_specs=(
            P("clip", "tm", None, None, None),
            P(),
            P(),
            P(),
            P(),
            P("clip", "tm", None, None, None),
        ),
        out_specs=(P("clip", "tm", None, None, None), P(), P(), P(), P()),
        check_vma=False,
    )
```

profile of v0, /device:TPU:0, one launch (start us, length us, event | category | flops | bytes accessed | tf_op | source)
XLA Modules:
  0.0 279.1 jit_solution(15549774472298984337)
XLA Ops:
  7.2 2.4 copy.71
  9.6 8.4 %all-to-all-start.2 = ((bf16[2,32,32,256]{3,2,0,1:T(8,128)(2,1)}), bf16[2,32,32,256]{3,2,0,1:T(8,128)(2,1)}, u32[]{:S(2)}, u32[]{:S(2)}) async-start(bf16[2,32,32,256]{3,2,0,1:T(8,128)(2,1)} %bitcast.205), calls=%async_computation.2 | async-start | bytes 2097152 | tf_op jit(solution)/shard_map/all_to_all | solution.py:136
  18.0 4.5 %fusion.86 = (bf16[2,32,1,32,1,128]{5,4,3,2,1,0:T(2,128)(2,1)S(1)}, bf16[2,32,1,32,1,128]{5,4,3,2,1,0:T(2,128)(2,1)S(1)}, bf16[2,32,1,32,1,128]{5,4,3,2,1,0:T(2,128)(2,1)S(1)}, bf16[2,32,1,32,1,128]{5,4,3,2,1,0:T(2,128)(2,1)S(1)}) fusion(bf16[2,32,2,32,2,128]{5,4,3,2,1,0:T(2,128)(2,1)S(1)} %bitcast.240), kind=kLoop, calls=%fused_computation.138 | loop fusion | bytes 4194304 | tf_op jit(solution)/shard_map/slice | solution.py:33
  22.6 0.4 fusion.40
  23.0 0.4 copy-done.11
  23.7 0.4 fusion.35
  24.1 1.8 fusion.32
  25.9 1.8 fusion.7
  27.7 0.4 convolution_add_fusion.4
  28.1 1.8 convolution_add_fusion.3
  29.9 1.7 convolution_add_fusion.1
  31.6 10.9 %all-to-all-done.2 = bf16[2,32,32,256]{3,2,0,1:T(8,128)(2,1)} async-done(((bf16[2,32,32,256]{3,2,0,1:T(8,128)(2,1)}), bf16[2,32,32,256]{3,2,0,1:T(8,128)(2,1)}, u32[]{:S(2)}, u32[]{:S(2)}) %all-to-all-start.2) | async-done | bytes 1048608 | tf_op jit(solution)/shard_map/all_to_all | solution.py:136
  42.5 1.3 copy.72
  43.9 0.9 copy-done.13
  44.8 0.5 fusion.12
  45.3 0.5 fusion.16
  45.7 1.6 add_convert_fusion.1
  47.3 5.9 %all-to-all-start.3 = ((bf16[32,2,32,256]{3,2,1,0:T(8,128)(2,1)}), bf16[32,2,32,256]{3,2,1,0:T(8,128)(2,1)}, u32[]{:S(2)}, u32[]{:S(2)}) async-start(bf16[32,2,32,256]{3,2,1,0:T(8,128)(2,1)} %add_convert_fusion.1), calls=%async_computation.3 | async-start | bytes 2097152 | tf_op jit(solution)/shard_map/all_to_all | solution.py:141
  53.2 2.1 pad_slice_fusion
  55.4 1.4 convolution_add_fusion
  57.1 0.6 copy-done.10
  57.7 1.8 fusion.84
  59.5 0.3 convolution_multiply_fusion.3
  60.0 0.3 multiply_reduce_fusion.2
  60.3 0.4 copy-done.22
  61.1 0.6 copy-done.32
  62.0 14.2 %all-to-all-done.3 = bf16[32,2,32,256]{3,2,1,0:T(8,128)(2,1)} async-done(((bf16[32,2,32,256]{3,2,1,0:T(8,128)(2,1)}), bf16[32,2,32,256]{3,2,1,0:T(8,128)(2,1)}, u32[]{:S(2)}, u32[]{:S(2)}) %all-to-all-start.3) | async-done | bytes 1048608 | tf_op jit(solution)/shard_map/all_to_all | solution.py:141
  76.2 1.5 copy.43
  77.8 3.2 %fusion.82 = (f32[256]{0:T(256)}, f32[2,256]{1,0:T(2,128)S(1)}, f32[2,32,32,256]{3,2,1,0:T(8,128)}, bf16[2,32,32,256]{3,2,1,0:T(8,128)(2,1)S(1)}) fusion(f32[256]{0:T(256)S(1)} %copy-done.17, f32[2,32,32,256]{3,2,1,0:T(8,128)S(1)} %get-tuple-element.40, f32[2,256]{1,0:T(2,128)S(1)} %fusion.23, f32[2,32,32,256]{3,2,1,0:T(8,128)S(1)} %bitcast.239, ...), kind=kLoop, calls=%fused_computation.136 | loop fusion | flops 9960704 | bytes 7349248 | tf_op jit(solution)/shard_map/transpose(jvp())/reduce_sum | solution.py:62
  81.0 0.3 fusion.6
  81.6 1.1 copy.36
  82.7 6.1 %all-to-all-start = ((bf16[2,32,32,256]{3,2,0,1:T(8,128)(2,1)}), bf16[2,32,32,256]{3,2,0,1:T(8,128)(2,1)}, u32[]{:S(2)}, u32[]{:S(2)}) async-start(bf16[2,32,32,256]{3,2,0,1:T(8,128)(2,1)} %copy.36), calls=%async_computation | async-start | bytes 2097152 | tf_op jit(solution)/shard_map/all_to_all | solution.py:135
  88.8 2.9 %multiply_reduce_fusion = (f32[256]{0:T(256)}, f32[2,256]{1,0:T(2,128)S(1)}) fusion(f32[2,32,32,256]{3,2,1,0:T(8,128)} %get-tuple-element.38, f32[2,32,32,256]{3,2,1,0:T(8,128)S(1)} %get-tuple-element.40, f32[2,256]{1,0:T(2,128)S(1)} %fusion.22, f32[2,256]{1,0:T(2,128)S(1)} %fusion.23, f32[2,256]{1,0:T(2,128)S(1)} %fusion.21, f32[256]{0:T(256)S(1)} %copy-done.17), kind=kLoop, calls=%fused_computation.16 | loop fusion | flops 5242112 | bytes 4204544 | tf_op jit(solution)/shard_map/transpose(jvp())/reduce_sum | solution.py:62
  91.8 0.3 convolution_multiply_fusion
  92.4 0.7 add_convert_fusion
  93.0 0.7 pad_slice_fusion.5
  93.8 0.3 copy-done.4
  94.1 0.5 convolution_bitcast_fusion.10
  94.8 0.5 convolution_bitcast_fusion.9
  95.3 0.5 convolution_bitcast_fusion.11
  95.9 0.5 convolution_bitcast_fusion.7
  96.4 0.5 convolution_bitcast_fusion.6
  96.9 0.5 convolution_bitcast_fusion.8
  97.4 0.8 maximum_bitcast_fusion.1
  98.1 0.5 convolution_bitcast_fusion.5
  98.6 0.5 convolution_bitcast_fusion.4
  99.1 0.5 convolution_bitcast_fusion.3
  99.6 0.8 maximum_bitcast_fusion.2
  100.4 11.3 %all-to-all-done = bf16[2,32,32,256]{3,2,0,1:T(8,128)(2,1)} async-done(((bf16[2,32,32,256]{3,2,0,1:T(8,128)(2,1)}), bf16[2,32,32,256]{3,2,0,1:T(8,128)(2,1)}, u32[]{:S(2)}, u32[]{:S(2)}) %all-to-all-start) | async-done | bytes 1048608 | tf_op jit(solution)/shard_map/all_to_all | solution.py:135
  111.7 1.3 copy.73
  113.1 0.4 fusion.14
  113.5 0.4 fusion.18
  114.0 1.5 add_convert_fusion.2
  115.5 6.2 %all-to-all-start.1 = ((bf16[32,2,32,256]{3,2,1,0:T(8,128)(2,1)}), bf16[32,2,32,256]{3,2,1,0:T(8,128)(2,1)}, u32[]{:S(2)}, u32[]{:S(2)}) async-start(bf16[32,2,32,256]{3,2,1,0:T(8,128)(2,1)} %add_convert_fusion.2), calls=%async_computation.1 | async-start | bytes 2097152 | tf_op jit(solution)/shard_map/all_to_all | solution.py:140
  121.7 2.1 pad_maximum_fusion
  124.1 0.5 convolution_bitcast_fusion.1
  124.6 0.5 convolution_bitcast_fusion
  125.0 2.0 convolution_bitcast_fusion.2
  127.1 0.9 pad_maximum_fusion.1
  128.1 43.7 %all-reduce.11 = (f32[256]{0:T(256)}, f32[256]{0:T(256)}) all-reduce(f32[256]{0:T(256)S(1)} %copy-done.19, f32[256]{0:T(256)S(1)} %copy-done.18), channel_id=1, replica_groups=mesh['clip'=2,'tm'=16] {'clip','tm'}, use_global_device_ids=true, to_apply=%region_6.7 | all-reduce | flops 512 | bytes 4096 | tf_op jit(solution)/shard_map/psum | solution.py:166
  171.7 94.6 %all-reduce.15.cloned.1.call-done = (f32[3,3,128,256]{2,3,1,0:T(8,128)}, f32[3,256,256]{2,1,0:T(8,128)}) async-done(((f32[3,3,128,256]{2,3,1,0:T(8,128)}, f32[3,256,256]{2,1,0:T(8,128)}), (f32[3,3,128,256]{2,3,1,0:T(8,128)}, f32[3,256,256]{2,1,0:T(8,128)})) %all-reduce.15.cloned.1.call-update) | async-done | bytes 1966096 | tf_op jit(solution)/shard_map/psum | solution.py:166
  266.4 2.7 copy.44
  269.1 2.3 copy.39
  271.4 0.9 copy.76
  (84 shorter events, 3.2 us)
Async XLA Ops:
  7.2 10.8 %copy-start.8 = (bf16[1,2,64,64,128]{4,3,2,1,0:T(8,128)(2,1)S(1)}, bf16[1,2,64,64,128]{4,3,2,1,0:T(8,128)(2,1)}, u32[]{:S(2)}) copy-start(bf16[1,2,64,64,128]{4,3,2,1,0:T(8,128)(2,1)} %param.6) | copy-start | bytes 6291460
  9.6 32.9 %all-to-all-start.2 = ((bf16[2,32,32,256]{3,2,0,1:T(8,128)(2,1)}), bf16[2,32,32,256]{3,2,0,1:T(8,128)(2,1)}, u32[]{:S(2)}, u32[]{:S(2)}) async-start(bf16[2,32,32,256]{3,2,0,1:T(8,128)(2,1)} %bitcast.205), calls=%async_computation.2 | async-start | bytes 2097152 | tf_op jit(solution)/shard_map/all_to_all | solution.py:136
  18.0 4.6 %copy-start.16 = (bf16[3,3,128,256]{3,2,1,0:T(8,128)(2,1)S(1)}, bf16[3,3,128,256]{3,2,1,0:T(8,128)(2,1)}, u32[]{:S(2)}) copy-start(bf16[3,3,128,256]{3,2,1,0:T(8,128)(2,1)} %param.7) | copy-start | bytes 1769476
  22.6 0.8 copy-start.11
  23.4 36.4 %copy-start.21 = (s32[256]{0:T(256)}, s32[256]{0:T(256)S(1)}, u32[]{:S(2)}) copy-start(s32[256]{0:T(256)S(1)} %get-tuple-element.52) | copy-start | bytes 3076
  23.4 36.4 %copy-start.25 = (s32[256]{0:T(256)}, s32[256]{0:T(256)S(1)}, u32[]{:S(2)}) copy-start(s32[256]{0:T(256)S(1)} %get-tuple-element.53) | copy-start | bytes 3076
  23.5 4.2 %copy-start.5 = (bf16[2,32,1,32,1,128]{5,3,4,2,1,0:T(8,128)(2,1)}, bf16[2,32,1,32,1,128]{5,3,4,2,1,0:T(8,128)(2,1)S(1)}, u32[]{:S(2)}) copy-start(bf16[2,32,1,32,1,128]{5,3,4,2,1,0:T(8,128)(2,1)S(1)} %copy.55) | copy-start | bytes 1572868
  23.6 4.6 %copy-start.3 = (bf16[2,32,1,32,1,128]{5,3,4,2,1,0:T(8,128)(2,1)}, bf16[2,32,1,32,1,128]{5,3,4,2,1,0:T(8,128)(2,1)S(1)}, u32[]{:S(2)}) copy-start(bf16[2,32,1,32,1,128]{5,3,4,2,1,0:T(8,128)(2,1)S(1)} %copy.56) | copy-start | bytes 1572868
  23.7 31.6 %copy-start = (bf16[2,32,1,32,1,128]{5,3,1,0,4,2:T(8,128)(2,1)}, bf16[2,32,1,32,1,128]{5,3,1,0,4,2:T(8,128)(2,1)S(1)}, u32[]{:S(2)}) copy-start(bf16[2,32,1,32,1,128]{5,3,1,0,4,2:T(8,128)(2,1)S(1)} %copy.57) | copy-start | bytes 1572868
  43.8 1.0 copy-start.13
  47.3 28.9 %all-to-all-start.3 = ((bf16[32,2,32,256]{3,2,1,0:T(8,128)(2,1)}), bf16[32,2,32,256]{3,2,1,0:T(8,128)(2,1)}, u32[]{:S(2)}, u32[]{:S(2)}) async-start(bf16[32,2,32,256]{3,2,1,0:T(8,128)(2,1)} %add_convert_fusion.1), calls=%async_computation.3 | async-start | bytes 2097152 | tf_op jit(solution)/shard_map/all_to_all | solution.py:141
  53.2 7.9 %copy-start.29 = (pred[256]{0:T(512)(128)(4,1)}, pred[256]{0:T(512)(128)(4,1)S(1)}, u32[]{:S(2)}) copy-start(pred[256]{0:T(512)(128)(4,1)S(1)} %compare_and_fusion) | copy-start | bytes 772
  53.2 2.2 copy-start.7
  55.4 1.6 copy-start.9
  55.4 2.3 copy-start.10
  60.0 0.7 copy-start.22
  60.0 0.8 copy-start.26
  60.8 16.9 %copy-start.17 = (f32[256]{0:T(256)S(1)}, f32[256]{0:T(256)}, u32[]{:S(2)}) copy-start(f32[256]{0:T(256)} %param.8) | copy-start | bytes 3076
  60.8 16.9 %copy-start.20 = (f32[256]{0:T(256)S(1)}, f32[256]{0:T(256)}, u32[]{:S(2)}) copy-start(f32[256]{0:T(256)} %param.9) | copy-start | bytes 3076
  61.1 0.6 copy-start.32
  77.7 3.3 %copy-start.23 = (s32[256]{0:T(256)S(1)}, s32[256]{0:T(256)}, u32[]{:S(2)}) copy-start(s32[256]{0:T(256)} %copy-done.21) | copy-start | bytes 3076
  77.7 3.3 %copy-start.27 = (s32[256]{0:T(256)S(1)}, s32[256]{0:T(256)}, u32[]{:S(2)}) copy-start(s32[256]{0:T(256)} %copy-done.25) | copy-start | bytes 3076
  77.7 3.3 %copy-start.30 = (pred[256]{0:T(512)(128)(4,1)S(1)}, pred[256]{0:T(512)(128)(4,1)}, u32[]{:S(2)}) copy-start(pred[256]{0:T(512)(128)(4,1)} %copy-done.29) | copy-start | bytes 772
  77.7 3.3 %copy-start.33 = (f32[2,32]{1,0:T(2,128)S(1)}, f32[2,32]{1,0:T(2,128)}, u32[]{:S(2)}) copy-start(f32[2,32]{1,0:T(2,128)} %copy-done.32) | copy-start | bytes 772
  82.7 28.9 %all-to-all-start = ((bf16[2,32,32,256]{3,2,0,1:T(8,128)(2,1)}), bf16[2,32,32,256]{3,2,0,1:T(8,128)(2,1)}, u32[]{:S(2)}, u32[]{:S(2)}) async-start(bf16[2,32,32,256]{3,2,0,1:T(8,128)(2,1)} %copy.36), calls=%async_computation | async-start | bytes 2097152 | tf_op jit(solution)/shard_map/all_to_all | solution.py:135
  88.8 3.0 %copy-start.24 = (s32[256]{0:T(256)S(1)}, s32[256]{0:T(256)}, u32[]{:S(2)}) copy-start(s32[256]{0:T(256)} %copy-done.21) | copy-start | bytes 3076
  88.8 3.0 %copy-start.28 = (s32[256]{0:T(256)S(1)}, s32[256]{0:T(256)}, u32[]{:S(2)}) copy-start(s32[256]{0:T(256)} %copy-done.25) | copy-start | bytes 3076
  88.8 3.0 %copy-start.31 = (pred[256]{0:T(512)(128)(4,1)S(1)}, pred[256]{0:T(512)(128)(4,1)}, u32[]{:S(2)}) copy-start(pred[256]{0:T(512)(128)(4,1)} %copy-done.29) | copy-start | bytes 772
  88.8 3.5 %copy-start.2 = (f32[2,32,32,256]{3,2,1,0:T(8,128)S(1)}, f32[2,32,32,256]{3,2,1,0:T(8,128)}, u32[]{:S(2)}) copy-start(f32[2,32,32,256]{3,2,1,0:T(8,128)} %get-tuple-element.38) | copy-start | bytes 6291460
  93.0 1.0 copy-start.4
  93.8 1.1 copy-start.1
  94.8 1.0 copy-start.12
  95.3 1.1 copy-start.6
  115.5 6.3 %copy-start.14 = (f32[1,3,128,256]{2,3,1,0:T(8,128)S(1)}, f32[1,3,128,256]{2,3,1,0:T(8,128)}, u32[]{:S(2)}) copy-start(f32[1,3,128,256]{2,3,1,0:T(8,128)} %maximum_bitcast_fusion.1) | copy-start | bytes 1179652
  115.5 153.6 %all-to-all-start.1 = ((bf16[32,2,32,256]{3,2,1,0:T(8,128)(2,1)}), bf16[32,2,32,256]{3,2,1,0:T(8,128)(2,1)}, u32[]{:S(2)}, u32[]{:S(2)}) async-start(bf16[32,2,32,256]{3,2,1,0:T(8,128)(2,1)} %add_convert_fusion.2), calls=%async_computation.1 | async-start | bytes 2097152 | tf_op jit(solution)/shard_map/all_to_all | solution.py:140
  121.7 144.7 %all-reduce.15.cloned.1.call-start = ((), (), s32[]{:S(2)}) async-start(), calls=%async_computation.4 | async-start | bytes 3932160 | tf_op jit(solution)/shard_map/psum | solution.py:166
  127.1 1.0 copy-start.18
  127.1 1.0 copy-start.19
  266.4 5.0 %copy-start.15 = (f32[3,256,256]{2,1,0:T(8,128)S(1)}, f32[3,256,256]{2,1,0:T(8,128)}, u32[]{:S(2)}) copy-start(f32[3,256,256]{2,1,0:T(8,128)} %get-tuple-element.58) | copy-start | bytes 2359300
Sparse Core Ops, SparseCore 0:
  128.5 137.7 all-reduce.14
where the time goes:
time: 280 us; the launch traced here: 279 us
  waiting for transfers between devices  131 us (47%)
  blocking collectives  43.7 us (16%)
  starting transfers between devices  26.6 us (10%)
  matrix products  25.9 us (9%)
  local copies, waits for them, and re-layouts  25.6 us (9%)
  between operations  14.6 us (5%)
  other arithmetic  11.8 us (4%)
    psum x1, waiting for transfers between devices, per_device(): lax.psum((spatial_part, gain_partial_sum, bias_part, temporal_part), ('cl...  94.6 us
    psum x1, blocking collectives, per_device(): lax.psum((spatial_part, gain_partial_sum, bias_part, temporal_part), ('cl...  43.7 us
    all_to_all x1, waiting for transfers between devices, per_device(): lax.all_to_all(act_grad_rows, 'tm', split_axis=0, concat_axis=1, tiled=True)  14.2 us
    dot_general x9, matrix products, per_device(): jnp.dot(phases[row_phase, col_phase], spatial_weight[row_offset, col_offs...  11.5 us
    all_to_all x1, waiting for transfers between devices, per_device(): lax.all_to_all(acts, 'tm', split_axis=1, concat_axis=0, tiled=True)  11.3 us
    all_to_all x1, waiting for transfers between devices, per_device(): lax.all_to_all(upstream, 'tm', split_axis=1, concat_axis=0, tiled=True)  10.9 us
    unnamed x75, local copies, waits for them, and re-layouts  10.3 us
    all_to_all x1, starting transfers between devices, per_device(): lax.all_to_all(upstream, 'tm', split_axis=1, concat_axis=0, tiled=True)  8.36 us
  transfers between devices with their start and end apart: 5, of which 4 were waited for; matrix products, arithmetic and copies ran while one was open for 14% of the time, Pallas kernels for 0%

commit v1 on v0

--- a/solution.py
+++ b/solution.py
@@ -138,7 +138,12 @@
         act_rows, grad_rows, temporal_weight, padded_lag
     )
     mixed = lax.all_to_all(mixed_rows, "tm", split_axis=0, concat_axis=1, tiled=True)
-    act_grad = lax.all_to_all(act_grad_rows, "tm", split_axis=0, concat_axis=1, tiled=True)
+    act_grad = jnp.concatenate(
+        lax.all_to_all(
+            jnp.stack(jnp.split(act_grad_rows, lax.axis_size("tm"), axis=0)), "tm", 0, 0
+        ),
+        axis=1,
+    )
     conv_grad, gain_partial_sum, bias_part = pullback(act_grad.astype(jnp.float32))
     conv_grad = conv_grad.astype(jnp.bfloat16)
     grad_versions = {

time: 280 us -> 290 us (1.036)
  local copies, waits for them, and re-layouts: 25.6 us -> 34.4 us
    unnamed x75 -> x84, local copies, waits for them, and re-layouts: 10.3 us -> 19.8 us
where the time goes in v1:
time: 290 us; the launch traced here: 289 us
  waiting for transfers between devices  131 us (45%)
  blocking collectives  43.5 us (15%)
  local copies, waits for them, and re-layouts  34.4 us (12%)
  starting transfers between devices  26.6 us (9%)
  matrix products  25.6 us (9%)
  between operations  14.6 us (5%)
  other arithmetic  13.4 us (5%)
    psum x1, waiting for transfers between devices, per_device(): lax.psum((spatial_part, gain_partial_sum, bias_part, temporal_part), ('cl...  94.6 us
    psum x1, blocking collectives, per_device(): lax.psum((spatial_part, gain_partial_sum, bias_part, temporal_part), ('cl...  43.5 us
    unnamed x84, local copies, waits for them, and re-layouts  19.8 us
    all_to_all x1, waiting for transfers between devices, per_device(): lax.all_to_all(jnp.stack(jnp.split(act_grad_rows, lax.axis_size('tm'), ax...  14.7 us
    dot_general x9, matrix products, per_device(): jnp.dot(phases[row_phase, col_phase], spatial_weight[row_offset, col_offs...  11.5 us
    all_to_all x1, waiting for transfers between devices, per_device(): lax.all_to_all(acts, 'tm', split_axis=1, concat_axis=0, tiled=True)  11.2 us
    all_to_all x1, waiting for transfers between devices, per_device(): lax.all_to_all(upstream, 'tm', split_axis=1, concat_axis=0, tiled=True)  10.9 us
    all_to_all x1, starting transfers between devices, per_device(): lax.all_to_all(upstream, 'tm', split_axis=1, concat_axis=0, tiled=True)  8.36 us
  transfers between devices with their start and end apart: 5, of which 4 were waited for; matrix products, arithmetic and copies ran while one was open for 14% of the time, Pallas kernels for 0%

profile of v1, /device:TPU:0, one launch (start us, length us, event | category | flops | bytes accessed | tf_op | source)
XLA Modules:
  0.0 289.5 jit_solution(6303809094886744038)
XLA Ops:
  7.2 2.4 copy.71
  9.6 8.4 %all-to-all-start.2 = ((bf16[2,32,32,256]{3,2,0,1:T(8,128)(2,1)}), bf16[2,32,32,256]{3,2,0,1:T(8,128)(2,1)}, u32[]{:S(2)}, u32[]{:S(2)}) async-start(bf16[2,32,32,256]{3,2,0,1:T(8,128)(2,1)} %bitcast.267), calls=%async_computation.2 | async-start | bytes 2097152 | tf_op jit(solution)/shard_map/all_to_all | solution.py:136
  18.0 4.5 %fusion.102 = (bf16[2,32,1,32,1,128]{5,4,3,2,1,0:T(2,128)(2,1)S(1)}, bf16[2,32,1,32,1,128]{5,4,3,2,1,0:T(2,128)(2,1)S(1)}, bf16[2,32,1,32,1,128]{5,4,3,2,1,0:T(2,128)(2,1)S(1)}, bf16[2,32,1,32,1,128]{5,4,3,2,1,0:T(2,128)(2,1)S(1)}) fusion(bf16[2,32,2,32,2,128]{5,4,3,2,1,0:T(2,128)(2,1)S(1)} %bitcast.302), kind=kLoop, calls=%fused_computation.171 | loop fusion | bytes 4194304 | tf_op jit(solution)/shard_map/slice | solution.py:33
  24.1 1.7 fusion.48
  25.9 1.8 fusion.7
  28.1 1.8 convolution_add_fusion.3
  29.9 1.7 convolution_add_fusion.1
  31.6 10.9 %all-to-all-done.2 = bf16[2,32,32,256]{3,2,0,1:T(8,128)(2,1)} async-done(((bf16[2,32,32,256]{3,2,0,1:T(8,128)(2,1)}), bf16[2,32,32,256]{3,2,0,1:T(8,128)(2,1)}, u32[]{:S(2)}, u32[]{:S(2)}) %all-to-all-start.2) | async-done | bytes 1048608 | tf_op jit(solution)/shard_map/all_to_all | solution.py:136
  42.5 1.3 copy.72
  43.9 0.9 copy-done.13
  45.7 0.6 add_convert_fusion.1
  46.3 0.6 fusion.45
  47.0 0.6 fusion.44
  47.6 0.6 fusion.43
  48.2 0.6 fusion.42
  48.9 0.6 fusion.41
  49.5 0.6 fusion.40
  50.1 0.6 fusion.39
  50.8 0.6 fusion.38
  51.4 0.6 fusion.37
  52.1 0.6 fusion.36
  52.7 0.6 fusion.35
  53.3 0.6 fusion.34
  54.0 0.6 fusion.33
  54.6 0.6 fusion.32
  55.2 0.6 fusion.31
  55.9 0.6 fusion.30
  56.5 5.9 %all-to-all-start.3 = ((bf16[16,2,2,32,256]{4,3,2,1,0:T(8,128)(2,1)}), bf16[16,2,2,32,256]{4,3,2,1,0:T(8,128)(2,1)}, u32[]{:S(2)}, u32[]{:S(2)}) async-start(bf16[16,2,2,32,256]{4,3,2,1,0:T(8,128)(2,1)} %fusion.30), calls=%async_computation.3 | async-start | bytes 2097152 | tf_op jit(solution)/shard_map/all_to_all | solution.py:142
  62.4 2.1 pad_slice_fusion
  64.6 1.4 convolution_add_fusion
  66.3 0.6 copy-done.10
  66.9 1.8 fusion.100
  69.9 0.5 copy-done.29
  70.7 14.7 %all-to-all-done.3 = bf16[16,2,2,32,256]{4,3,2,1,0:T(8,128)(2,1)} async-done(((bf16[16,2,2,32,256]{4,3,2,1,0:T(8,128)(2,1)}), bf16[16,2,2,32,256]{4,3,2,1,0:T(8,128)(2,1)}, u32[]{:S(2)}, u32[]{:S(2)}) %all-to-all-start.3) | async-done | bytes 1048608 | tf_op jit(solution)/shard_map/all_to_all | solution.py:142
  85.4 1.5 convert_bitcast_fusion
  87.6 3.2 %fusion.98 = (f32[256]{0:T(256)}, f32[2,256]{1,0:T(2,128)S(1)}, f32[2,32,32,256]{3,2,1,0:T(8,128)}, bf16[2,32,32,256]{3,2,1,0:T(8,128)(2,1)S(1)}) fusion(f32[256]{0:T(256)S(1)} %copy-done.17, f32[2,32,32,256]{3,2,1,0:T(8,128)S(1)} %get-tuple-element.40, f32[2,256]{1,0:T(2,128)S(1)} %fusion.23, f32[2,32,32,256]{3,2,1,0:T(8,128)S(1)} %bitcast.301, ...), kind=kLoop, calls=%fused_computation.169 | loop fusion | flops 9960704 | bytes 7349248 | tf_op jit(solution)/shard_map/transpose(jvp())/reduce_sum | solution.py:62
  91.2 0.9 fusion.21
  92.1 1.1 copy.36
  93.3 6.1 %all-to-all-start = ((bf16[2,32,32,256]{3,2,0,1:T(8,128)(2,1)}), bf16[2,32,32,256]{3,2,0,1:T(8,128)(2,1)}, u32[]{:S(2)}, u32[]{:S(2)}) async-start(bf16[2,32,32,256]{3,2,0,1:T(8,128)(2,1)} %copy.36), calls=%async_computation | async-start | bytes 2097152 | tf_op jit(solution)/shard_map/all_to_all | solution.py:135
  99.4 3.0 %multiply_reduce_fusion = (f32[256]{0:T(256)}, f32[2,256]{1,0:T(2,128)S(1)}) fusion(f32[2,32,32,256]{3,2,1,0:T(8,128)} %get-tuple-element.38, f32[2,32,32,256]{3,2,1,0:T(8,128)S(1)} %get-tuple-element.40, f32[2,256]{1,0:T(2,128)S(1)} %fusion.22, f32[2,256]{1,0:T(2,128)S(1)} %fusion.23, f32[2,256]{1,0:T(2,128)S(1)} %fusion.21, f32[256]{0:T(256)S(1)} %copy-done.17), kind=kLoop, calls=%fused_computation.17 | loop fusion | flops 5242112 | bytes 4204544 | tf_op jit(solution)/shard_map/transpose(jvp())/reduce_sum | solution.py:62
  103.0 0.7 add_convert_fusion
  103.6 0.7 pad_slice_fusion.5
  105.5 0.5 convolution_bitcast_fusion.9
  105.9 0.5 convolution_bitcast_fusion.11
  106.5 0.5 convolution_bitcast_fusion.7
  107.0 0.5 convolution_bitcast_fusion.6
  107.5 0.5 convolution_bitcast_fusion.8
  108.0 0.8 maximum_bitcast_fusion.1
  108.8 0.5 convolution_bitcast_fusion.5
  109.2 0.5 convolution_bitcast_fusion.4
  109.7 0.5 convolution_bitcast_fusion.3
  110.2 0.8 maximum_bitcast_fusion.2
  111.0 11.2 %all-to-all-done = bf16[2,32,32,256]{3,2,0,1:T(8,128)(2,1)} async-done(((bf16[2,32,32,256]{3,2,0,1:T(8,128)(2,1)}), bf16[2,32,32,256]{3,2,0,1:T(8,128)(2,1)}, u32[]{:S(2)}, u32[]{:S(2)}) %all-to-all-start) | async-done | bytes 1048608 | tf_op jit(solution)/shard_map/all_to_all | solution.py:135
  122.2 1.3 copy.73
  124.5 1.5 add_convert_fusion.2
  126.0 6.2 %all-to-all-start.1 = ((bf16[32,2,32,256]{3,2,1,0:T(8,128)(2,1)}), bf16[32,2,32,256]{3,2,1,0:T(8,128)(2,1)}, u32[]{:S(2)}, u32[]{:S(2)}) async-start(bf16[32,2,32,256]{3,2,1,0:T(8,128)(2,1)} %add_convert_fusion.2), calls=%async_computation.1 | async-start | bytes 2097152 | tf_op jit(solution)/shard_map/all_to_all | solution.py:140
  132.3 2.1 pad_maximum_fusion
  135.6 2.0 convolution_bitcast_fusion.2
  137.6 0.9 pad_maximum_fusion.1
  138.6 43.5 %all-reduce.11 = (f32[256]{0:T(256)}, f32[256]{0:T(256)}) all-reduce(f32[256]{0:T(256)S(1)} %copy-done.19, f32[256]{0:T(256)S(1)} %copy-done.18), channel_id=1, replica_groups=mesh['clip'=2,'tm'=16] {'clip','tm'}, use_global_device_ids=true, to_apply=%region_6.7 | all-reduce | flops 512 | bytes 4096 | tf_op jit(solution)/shard_map/psum | solution.py:171
  182.1 94.6 %all-reduce.15.cloned.1.call-done = (f32[3,3,128,256]{2,3,1,0:T(8,128)}, f32[3,256,256]{2,1,0:T(8,128)}) async-done(((f32[3,3,128,256]{2,3,1,0:T(8,128)}, f32[3,256,256]{2,1,0:T(8,128)}), (f32[3,3,128,256]{2,3,1,0:T(8,128)}, f32[3,256,256]{2,1,0:T(8,128)})) %all-reduce.15.cloned.1.call-update) | async-done | bytes 1966096 | tf_op jit(solution)/shard_map/psum | solution.py:171
  276.7 2.7 copy.44
  279.4 2.3 copy.39
  281.7 0.9 copy.91
  (95 shorter events, 9.8 us)
Async XLA Ops:
  7.2 10.8 %copy-start.8 = (bf16[1,2,64,64,128]{4,3,2,1,0:T(8,128)(2,1)S(1)}, bf16[1,2,64,64,128]{4,3,2,1,0:T(8,128)(2,1)}, u32[]{:S(2)}) copy-start(bf16[1,2,64,64,128]{4,3,2,1,0:T(8,128)(2,1)} %param.6) | copy-start | bytes 6291460
  9.6 32.9 %all-to-all-start.2 = ((bf16[2,32,32,256]{3,2,0,1:T(8,128)(2,1)}), bf16[2,32,32,256]{3,2,0,1:T(8,128)(2,1)}, u32[]{:S(2)}, u32[]{:S(2)}) async-start(bf16[2,32,32,256]{3,2,0,1:T(8,128)(2,1)} %bitcast.267), calls=%async_computation.2 | async-start | bytes 2097152 | tf_op jit(solution)/shard_map/all_to_all | solution.py:136
  18.0 4.6 %copy-start.16 = (bf16[3,3,128,256]{3,2,1,0:T(8,128)(2,1)S(1)}, bf16[3,3,128,256]{3,2,1,0:T(8,128)(2,1)}, u32[]{:S(2)}) copy-start(bf16[3,3,128,256]{3,2,1,0:T(8,128)(2,1)} %param.7) | copy-start | bytes 1769476
  22.6 0.8 copy-start.11
  23.4 46.5 %copy-start.23 = (s32[256]{0:T(256)}, s32[256]{0:T(256)S(1)}, u32[]{:S(2)}) copy-start(s32[256]{0:T(256)S(1)} %get-tuple-element.53) | copy-start | bytes 3076
  23.4 67.5 %copy-start.21 = (s32[256]{0:T(256)}, s32[256]{0:T(256)S(1)}, u32[]{:S(2)}) copy-start(s32[256]{0:T(256)S(1)} %get-tuple-element.52) | copy-start | bytes 3076
  23.5 4.2 %copy-start.5 = (bf16[2,32,1,32,1,128]{5,3,4,2,1,0:T(8,128)(2,1)}, bf16[2,32,1,32,1,128]{5,3,4,2,1,0:T(8,128)(2,1)S(1)}, u32[]{:S(2)}) copy-start(bf16[2,32,1,32,1,128]{5,3,4,2,1,0:T(8,128)(2,1)S(1)} %copy.55) | copy-start | bytes 1572868
  23.6 4.5 %copy-start.3 = (bf16[2,32,1,32,1,128]{5,3,4,2,1,0:T(8,128)(2,1)}, bf16[2,32,1,32,1,128]{5,3,4,2,1,0:T(8,128)(2,1)S(1)}, u32[]{:S(2)}) copy-start(bf16[2,32,1,32,1,128]{5,3,4,2,1,0:T(8,128)(2,1)S(1)} %copy.56) | copy-start | bytes 1572868
  23.7 40.8 %copy-start = (bf16[2,32,1,32,1,128]{5,3,1,0,4,2:T(8,128)(2,1)}, bf16[2,32,1,32,1,128]{5,3,1,0,4,2:T(8,128)(2,1)S(1)}, u32[]{:S(2)}) copy-start(bf16[2,32,1,32,1,128]{5,3,1,0,4,2:T(8,128)(2,1)S(1)} %copy.57) | copy-start | bytes 1572868
  43.8 1.0 copy-start.13
  56.5 28.9 %all-to-all-start.3 = ((bf16[16,2,2,32,256]{4,3,2,1,0:T(8,128)(2,1)}), bf16[16,2,2,32,256]{4,3,2,1,0:T(8,128)(2,1)}, u32[]{:S(2)}, u32[]{:S(2)}) async-start(bf16[16,2,2,32,256]{4,3,2,1,0:T(8,128)(2,1)} %fusion.30), calls=%async_computation.3 | async-start | bytes 2097152 | tf_op jit(solution)/shard_map/all_to_all | solution.py:142
  62.4 7.4 %copy-start.26 = (pred[256]{0:T(512)(128)(4,1)}, pred[256]{0:T(512)(128)(4,1)S(1)}, u32[]{:S(2)}) copy-start(pred[256]{0:T(512)(128)(4,1)S(1)} %compare_and_fusion) | copy-start | bytes 772
  62.4 2.2 copy-start.7
  64.6 1.6 copy-start.9
  64.6 2.3 copy-start.10
  69.9 0.6 copy-start.29
  86.9 0.7 copy-start.17
  86.9 0.7 copy-start.20
  87.6 3.3 %copy-start.24 = (s32[256]{0:T(256)S(1)}, s32[256]{0:T(256)}, u32[]{:S(2)}) copy-start(s32[256]{0:T(256)} %copy-done.23) | copy-start | bytes 3076
  87.6 3.3 %copy-start.27 = (pred[256]{0:T(512)(128)(4,1)S(1)}, pred[256]{0:T(512)(128)(4,1)}, u32[]{:S(2)}) copy-start(pred[256]{0:T(512)(128)(4,1)} %copy-done.26) | copy-start | bytes 772
  87.6 3.3 %copy-start.30 = (f32[2,32]{1,0:T(2,128)S(1)}, f32[2,32]{1,0:T(2,128)}, u32[]{:S(2)}) copy-start(f32[2,32]{1,0:T(2,128)} %copy-done.29) | copy-start | bytes 772
  93.3 28.9 %all-to-all-start = ((bf16[2,32,32,256]{3,2,0,1:T(8,128)(2,1)}), bf16[2,32,32,256]{3,2,0,1:T(8,128)(2,1)}, u32[]{:S(2)}, u32[]{:S(2)}) async-start(bf16[2,32,32,256]{3,2,0,1:T(8,128)(2,1)} %copy.36), calls=%async_computation | async-start | bytes 2097152 | tf_op jit(solution)/shard_map/all_to_all | solution.py:135
  99.3 3.1 %copy-start.22 = (s32[256]{0:T(256)S(1)}, s32[256]{0:T(256)}, u32[]{:S(2)}) copy-start(s32[256]{0:T(256)} %copy-done.21) | copy-start | bytes 3076
  99.3 3.1 %copy-start.25 = (s32[256]{0:T(256)S(1)}, s32[256]{0:T(256)}, u32[]{:S(2)}) copy-start(s32[256]{0:T(256)} %copy-done.23) | copy-start | bytes 3076
  99.4 3.0 %copy-start.28 = (pred[256]{0:T(512)(128)(4,1)S(1)}, pred[256]{0:T(512)(128)(4,1)}, u32[]{:S(2)}) copy-start(pred[256]{0:T(512)(128)(4,1)} %copy-done.26) | copy-start | bytes 772
  99.4 3.6 %copy-start.2 = (f32[2,32,32,256]{3,2,1,0:T(8,128)S(1)}, f32[2,32,32,256]{3,2,1,0:T(8,128)}, u32[]{:S(2)}) copy-start(f32[2,32,32,256]{3,2,1,0:T(8,128)} %get-tuple-element.38) | copy-start | bytes 6291460
  103.6 1.0 copy-start.4
  104.4 1.1 copy-start.1
  105.4 1.0 copy-start.12
  105.9 1.1 copy-start.6
  126.0 6.3 %copy-start.14 = (f32[1,3,128,256]{2,3,1,0:T(8,128)S(1)}, f32[1,3,128,256]{2,3,1,0:T(8,128)}, u32[]{:S(2)}) copy-start(f32[1,3,128,256]{2,3,1,0:T(8,128)} %maximum_bitcast_fusion.1) | copy-start | bytes 1179652
  126.0 153.4 %all-to-all-start.1 = ((bf16[32,2,32,256]{3,2,1,0:T(8,128)(2,1)}), bf16[32,2,32,256]{3,2,1,0:T(8,128)(2,1)}, u32[]{:S(2)}, u32[]{:S(2)}) async-start(bf16[32,2,32,256]{3,2,1,0:T(8,128)(2,1)} %add_convert_fusion.2), calls=%async_computation.1 | async-start | bytes 2097152 | tf_op jit(solution)/shard_map/all_to_all | solution.py:140
  132.2 144.5 %all-reduce.15.cloned.1.call-start = ((), (), s32[]{:S(2)}) async-start(), calls=%async_computation.4 | async-start | bytes 3932160 | tf_op jit(solution)/shard_map/psum | solution.py:171
  137.6 1.0 copy-start.18
  137.6 1.0 copy-start.19
  276.7 5.0 %copy-start.15 = (f32[3,256,256]{2,1,0:T(8,128)S(1)}, f32[3,256,256]{2,1,0:T(8,128)}, u32[]{:S(2)}) copy-start(f32[3,256,256]{2,1,0:T(8,128)} %get-tuple-element.58) | copy-start | bytes 2359300
Sparse Core Ops, SparseCore 0:
  139.0 137.5 all-reduce.14
